TPU v7x, 32 devices: a whole 2x2x4 slice. The times are simulated.
32 devices in a mesh: px: 4 (over x, core), py: 8 (over z, y).
Axes of the slice: x: 2, y: 2, z: 4, core: 2. Of those that a mesh axis runs over, the one named last changes fastest.
Arguments:
- field: float32 [256, 256, 256], P('px', 'py'), may hold values from -6 to 6
- diffusivity: bfloat16 [256, 256, 256], P('px', 'py'), may hold values from 0.049804688 to 1
- velocity: bfloat16 [3, 256, 256, 256], P(None, 'px', 'py'), may hold values from -4 to 4
- margin: int32 [4, 2], P('px'), may hold values from 0 to 4, as said below
Outputs:
- advected: float32 [256, 256, 256], P('px', 'py')
- controls: float32 [128, 128, 128], P('px', 'py')
Inputs may be any that keep to these rules, and one draw needn't show every extreme that they name: One subdomain has an upper margin of 0 and one has a lower margin of 4.
All inputs are finite; a program needn't handle non-finite values.
Results may differ from a plain program's by a relative error of at most 0.0003.
Values may be sent and summed in bfloat16 or wider, within the bound.
A program may use at most 192 MiB of HBM per device.

v0:
```python
import functools

import jax
import jax.numpy as jnp
import numpy as np
from jax import lax
from jax.experimental import pallas as pl
from jax.experimental.pallas import tpu as pltpu
from jax.sharding import PartitionSpec as P

STEPS = 4
OVMAX = 4
HALO = 8
QROWS = 24
HIGH = lax.Precision.HIGHEST
MESH = pl.DeviceIdType.MESH


def bspline(t):
    t = np.abs(t)
    inner = (4.0 - 6.0 * t * t + 3.0 * t**3) / 6.0
    outer = np.maximum(2.0 - t, 0.0) ** 3 / 6.0
    return np.where(t < 1.0, inner, outer)


def basis(total):
    j = np.arange(total, dtype=np.float64)[:, None]
    k = np.arange(total // 2, dtype=np.float64)[None, :]
    return bspline(0.5 * (j - 2.0 * k - 0.5))


TAPS = [float(bspline(0.5 * (j - 3.5))) for j in range(8)]


def z_matrix(total):
    table = basis(total)
    return np.linalg.solve(table.T @ table, table.T).T.astype(np.float32)


def y_matrix(total, count):
    table = basis(total)
    inverse = np.linalg.inv(table.T @ table)
    ctrl = total // 2
    own = ctrl // count
    result = np.zeros((ctrl, count, QROWS))
    for p in range(count):
        for q in range(own + 4):
            k = own * p - 2 + q
            if 0 <= k < ctrl:
                result[:, p, q] = inverse[:, k]
    return result.reshape(ctrl, count * QROWS).astype(np.float32)


def schwarz_table(total, count):
    table = basis(total)
    gram = table.T @ table
    ctrl = total // 2
    block = ctrl // count
    width = block + 2 * OVMAX
    out = np.zeros((3, OVMAX + 1, OVMAX + 1, 2, block, block + 2 * HALO))
    for kind, p in enumerate((0, min(1, count - 1), count - 1)):
        start = p * block
        knots = start - OVMAX + np.arange(width)
        near = start - HALO + np.arange(block + 2 * HALO)

        def pick(rows, cols):
            good = ((rows >= 0) & (rows < ctrl))[:, None] & ((cols >= 0) & (cols < ctrl))[None, :]
            return np.where(good, gram[np.clip(rows, 0, ctrl - 1)][:, np.clip(cols, 0, ctrl - 1)], 0.0)

        full, rows = pick(knots, knots), pick(knots, near)
        for low in range(OVMAX + 1):
            for up in range(OVMAX + 1):
                weight = (knots >= start - low) & (knots < start + block + up) & (knots >= 0) & (knots < ctrl)
                weight = weight.astype(np.float64)
                local = full * weight[:, None] * weight[None, :] + np.diag(1.0 - weight)
                own = (np.linalg.inv(local) * weight[None, :])[OVMAX : OVMAX + block]
                out[kind, low, up, 0, :, :width] = own
                out[kind, low, up, 1] = own @ rows
    return out.reshape(-1, 2 * block, block + 2 * HALO).astype(np.float32)


def kernel(
    nx, ny, cx, cy, nz, chunks,
    margin, field, kappa, velo, zmat_h, ymat_h, tab_h,
    adv, ctrl_out,
    U, kb, vb, kk, ky, kz, hx, hy, hz, hzp, ys, yr, gy, kxr, hxr,
    xps, xpr, xc, zf, a2s, a2r, bs, rh, ce, zmat, ymat, tab,
    in_sem, cst_sem, xs_sem, xr_sem, ki_s, ki_r, ys_sem, yr_sem, ps_sem, pr_sem,
    as_sem, ar_sem, bs_sem, br_sem, hs_sem, hr_sem, cs_sem, cr_sem,
):
    px, py = lax.axis_index("px"), lax.axis_index("py")
    rows = cx // chunks
    block = cx // 2
    mine = block // ny
    own = cy // 2
    zc = nz // 2

    loads = [
        pltpu.make_async_copy(kappa, kb, in_sem.at[0]),
        pltpu.make_async_copy(velo, vb, in_sem.at[1]),
        pltpu.make_async_copy(field, U.at[0, pl.ds(1, cx)], in_sem.at[2]),
    ]
    consts = [
        pltpu.make_async_copy(zmat_h, zmat, cst_sem.at[0]),
        pltpu.make_async_copy(ymat_h, ymat, cst_sem.at[1]),
        pltpu.make_async_copy(tab_h, tab, cst_sem.at[2]),
    ]
    for c in loads + consts:
        c.start()

    zero_face = jnp.zeros((cy, nz), jnp.float32)
    for s in range(2):
        U[s, 0] = zero_face
        U[s, cx + 1] = zero_face
        kxr[s] = jnp.zeros((cy, nz), kxr.dtype)
        hxr[s] = jnp.zeros((cy, nz), hxr.dtype)
        xpr[s] = jnp.zeros((2, cy, nz), jnp.float32)
    yr[...] = jnp.zeros(yr.shape, jnp.float32)
    rh[...] = jnp.zeros(rh.shape, jnp.float32)
    ce[0:HALO] = jnp.zeros((HALO, own * zc), jnp.float32)
    ce[HALO + block :] = jnp.zeros((HALO, own * zc), jnp.float32)
    zf[...] = jnp.zeros(zf.shape, jnp.float32)

    barrier = pltpu.get_barrier_semaphore()

    @pl.loop(1, ny)
    def _(d):
        pl.semaphore_signal(barrier, inc=1, device_id=(px, lax.rem(py + d, ny)), device_id_type=MESH)

    has = {0: px > 0, 1: px < nx - 1}
    to = {0: (px - 1, py), 1: (px + 1, py)}
    hasy = {0: py > 0, 1: py < ny - 1}
    toy = {0: (px, py - 1), 1: (px, py + 1)}
    for side in (0, 1):

        @pl.when(has[side])
        def _(side=side):
            pl.semaphore_signal(barrier, inc=1, device_id=to[side], device_id_type=MESH)

    neighbours = jnp.where(px > 0, 1, 0) + jnp.where(px < nx - 1, 1, 0)
    pl.semaphore_wait(barrier, ny - 1 + neighbours)

    def remote(src, dst, ss, rs, dev):
        return pltpu.make_async_remote_copy(
            src_ref=src, dst_ref=dst, send_sem=ss, recv_sem=rs, device_id=dev, device_id_type=MESH
        )

    def x_init(side):
        edge = 0 if side == 0 else cx - 1
        return [
            remote(kappa.at[edge], kxr.at[1 - side], ki_s.at[0, side], ki_r.at[0, 1 - side], to[side]),
            remote(velo.at[0, edge], hxr.at[1 - side], ki_s.at[1, side], ki_r.at[1, 1 - side], to[side]),
            remote(
                field.at[edge],
                U.at[0, cx + 1 if side == 0 else 0],
                xs_sem.at[0, side],
                xr_sem.at[0, 1 - side],
                to[side],
            ),
        ]

    def x_face(t, side):
        slot = t % 2
        return remote(
            U.at[slot, 1 if side == 0 else cx],
            U.at[slot, cx + 1 if side == 0 else 0],
            xs_sem.at[t, side],
            xr_sem.at[t, 1 - side],
            to[side],
        )

    def y_face(t, c, side):
        items = pl.ds(0, 3) if t == 0 else pl.ds(t + 2, 1)
        part = pl.ds(c * rows, rows)
        return remote(
            ys.at[side, items, part],
            yr.at[1 - side, items, part],
            ys_sem.at[t, c, side],
            yr_sem.at[t, c, 1 - side],
            toy[side],
        )

    def y_arrival(t, c, side):
        items = pl.ds(0, 3) if t == 0 else pl.ds(t + 2, 1)
        part = pl.ds(c * rows, rows)
        return remote(
            ys.at[side, items, part],
            yr.at[side, items, part],
            ys_sem.at[t, c, side],
            yr_sem.at[t, c, side],
            toy[side],
        )

    def x_arrival(t, side):
        slot = t % 2
        return remote(
            U.at[slot, 1],
            U.at[slot, 0 if side == 0 else cx + 1],
            xs_sem.at[t, side],
            xr_sem.at[t, side],
            to[side],
        )

    def when_do(cond, do):
        pl.when(cond)(do)

    for side in (0, 1):

        @pl.when(has[side])
        def _(side=side):
            for c in x_init(side):
                c.start()

    for c in loads:
        c.wait()

    lane = lax.broadcasted_iota(jnp.int32, (cy, nz), 1)
    row = lax.broadcasted_iota(jnp.int32, (cy, nz), 0)
    last_lane, first_lane = lane == nz - 1, lane == 0
    last_row, first_row = row == cy - 1, row == 0

    def prepare(x):
        k = kb[x].astype(jnp.float32) * 0.05
        kk[x + 1] = k
        ky[x] = k + pltpu.roll(k, cy - 1, 0)
        kz[x] = k + jnp.where(last_lane, 0.0, pltpu.roll(k, nz - 1, 1))
        hx[x + 1] = vb[0, x].astype(jnp.float32) * 0.025
        h = vb[1, x].astype(jnp.float32) * 0.025
        hy[x] = h
        g = vb[2, x].astype(jnp.float32) * 0.025
        hz[x] = g
        hzp[x] = jnp.where(last_lane, 0.0, pltpu.roll(g, nz - 1, 1))
        u = U[0, x + 1]
        at = pl.ds(x, 1)
        for side, pick in ((0, slice(0, 1)), (1, slice(cy - 1, cy))):
            ys[side, 0, at] = k[pick]
            ys[side, 1, at] = h[pick]
            ys[side, 2, at] = u[pick]

    for c in range(chunks):

        @pl.loop(0, rows)
        def _(i, c=c):
            prepare(c * rows + i)

        for side in (0, 1):
            when_do(hasy[side], lambda c=c, side=side: y_face(0, c, side).start())

    for side in (0, 1):

        @pl.when(has[side])
        def _(side=side):
            remote(kappa.at[0], kxr.at[side], ki_s.at[0, side], ki_r.at[0, side], to[side]).wait_recv()
            remote(velo.at[0, 0], hxr.at[side], ki_s.at[1, side], ki_r.at[1, side], to[side]).wait_recv()

        at = 0 if side == 0 else cx + 1
        kk[at] = kxr[side].astype(jnp.float32) * 0.05
        hx[at] = hxr[side].astype(jnp.float32) * 0.025

    def x_flux(s, x):
        u, up = U[s, x], U[s, x + 1]
        return (kk[x] + kk[x + 1]) * (up - u) - (hx[x] * (u * u) + hx[x + 1] * (up * up))

    def partial(side):
        for q in range(2):
            k = (q - 2) if side == 0 else block + q
            total = None
            for j in range(8):
                i = 2 * k - 3 + j
                if 0 <= i < cx:
                    term = TAPS[j] * adv[i]
                    total = term if total is None else total + term
            xps[side, q] = total
        return remote(xps.at[side], xpr.at[1 - side], ps_sem.at[side], pr_sem.at[1 - side], to[side])

    order = [0, chunks - 1] + list(range(1, chunks - 1)) if chunks > 1 else [0]
    for t in range(STEPS):
        s = t % 2
        last = t == STEPS - 1
        for c in order:
            if c == 0:
                when_do(has[0], lambda t=t: x_arrival(t, 0).wait_recv())
            if c == chunks - 1:
                when_do(has[1], lambda t=t: x_arrival(t, 1).wait_recv())
            for side in (0, 1):
                when_do(hasy[side], lambda t=t, c=c, side=side: y_arrival(t, c, side).wait_recv())
            part = pl.ds(c * rows, rows)
            for side in (0, 1):
                a, b = ys[side, t + 2, part], yr[side, t + 2, part]
                diff = (a - b) if side == 0 else (b - a)
                gy[side, part] = (ys[side, 0, part] + yr[side, 0, part]) * diff - (
                    ys[side, 1, part] * (a * a) + yr[side, 1, part] * (b * b)
                )

            def line(i, flux, t=t, s=s, c=c, last=last):
                x = c * rows + i
                u, k = U[s, x + 1], kk[x + 1]
                up = U[s, x + 2]
                sq = u * u
                gx = (k + kk[x + 2]) * (up - u) - (hx[x + 1] * sq + hx[x + 2] * (up * up))
                fy = hy[x] * sq
                g = ky[x] * (pltpu.roll(u, cy - 1, 0) - u) - (fy + pltpu.roll(fy, cy - 1, 0))
                at = pl.ds(x, 1)
                g = jnp.where(last_row, gy[1, at], g)
                gym = jnp.where(first_row, gy[0, at], pltpu.roll(g, 1, 0))
                uz = jnp.where(last_lane, 0.0, pltpu.roll(u, nz - 1, 1))
                fz = hz[x] * sq
                gz = kz[x] * (uz - u) - (fz + hzp[x] * (uz * uz))
                gzm = jnp.where(first_lane, k * u - fz, pltpu.roll(gz, 1, 1))
                new = u + ((gx - flux) + (g - gym) + (gz - gzm))
                if last:
                    adv[x] = new
                else:
                    U[1 - s, x + 1] = new
                    ys[0, t + 3, at] = new[0:1]
                    ys[1, t + 3, at] = new[cy - 1 : cy]
                return gx

            lax.fori_loop(0, rows, line, x_flux(s, c * rows))
            if not last:
                for side in (0, 1):
                    when_do(hasy[side], lambda t=t, c=c, side=side: y_face(t + 1, c, side).start())
                if c == 0:
                    when_do(has[0], lambda t=t: x_face(t + 1, 0).start())
                if c == chunks - 1:
                    when_do(has[1], lambda t=t: x_face(t + 1, 1).start())
            else:
                for side, at in ((0, 0), (1, chunks - 1)):
                    if c == at:
                        copy = partial(side)
                        when_do(has[side], lambda copy=copy: copy.start())
        for side in (0, 1):

            @pl.when(has[side])
            def _(t=t, side=side):
                x_face(t, side).wait_send()
                if t == 0:
                    for c in x_init(side)[:2]:
                        c.wait_send()

            @pl.when(hasy[side])
            def _(t=t, side=side):
                for c in range(chunks):
                    y_face(t, c, side).wait_send()

    def x_row(k, low, high):
        total = None
        for j in range(8):
            if low <= j < high:
                term = TAPS[j] * adv[2 * k - 3 + j]
                total = term if total is None else total + term
        return total

    for k in (0, 1):
        xc[k] = x_row(k, 3 - 2 * k, 8)
    for k in (block - 2, block - 1):
        xc[k] = x_row(k, 0, cx - 2 * k + 3)

    @pl.loop(2, block - 2)
    def _(k):
        xc[k] = x_row(k, 0, 8)

    for side in (0, 1):

        @pl.when(has[side])
        def _(side=side):
            c = remote(xps.at[side], xpr.at[side], ps_sem.at[side], pr_sem.at[side], to[side])
            c.wait()

        for q in range(2):
            k = q if side == 0 else block - 2 + q
            xc[k] += xpr[side, q]

    for c in consts:
        c.wait()

    def group(peer):
        first = peer * mine
        lines = xc[pl.ds(first, mine)].reshape(mine * cy, nz)
        fitted = jnp.dot(lines, zmat[...], precision=HIGH, preferred_element_type=jnp.float32)
        zf[:, 8 : 8 + cy, :] = fitted.reshape(mine, cy, zc)
        for a in range(mine):
            total = None
            for j in range(8):
                term = TAPS[j] * zf[a, pl.ds(1 + j, QROWS, stride=2), :]
                total = term if total is None else total + term
            a2s[peer, a] = total

    def a2a(peer):
        return remote(a2s.at[peer], a2r.at[py], as_sem.at[peer], ar_sem.at[py], (px, peer))

    @pl.loop(1, ny)
    def _(d):
        peer = lax.rem(py + d, ny)
        group(peer)
        a2a(peer).start()

    group(py)
    a2r[py] = a2s[py]

    @pl.loop(1, ny)
    def _(d):
        peer = lax.rem(py + d, ny)
        remote(a2s.at[peer], a2r.at[peer], as_sem.at[peer], ar_sem.at[peer], (px, peer)).wait()

    gathered = jnp.concatenate([a2r[:, a].reshape(ny * QROWS, zc) for a in range(mine)], axis=1)
    solved = jnp.dot(ymat[...], gathered, precision=HIGH, preferred_element_type=jnp.float32)
    for q in range(ny):
        for a in range(mine):
            bs[q, a * own : (a + 1) * own] = solved[q * own : (q + 1) * own, a * zc : (a + 1) * zc]

    span = mine * own
    base = OVMAX * own

    def back(peer):
        return remote(
            bs.at[peer], rh.at[pl.ds(base + py * span, span)], bs_sem.at[peer], br_sem.at[py], (px, peer)
        )

    @pl.loop(1, ny)
    def _(d):
        back(lax.rem(py + d, ny)).start()

    rh[pl.ds(base + py * span, span)] = bs[py]

    @pl.loop(1, ny)
    def _(d):
        peer = lax.rem(py + d, ny)
        remote(
            bs.at[peer], rh.at[pl.ds(base + peer * span, span)], bs_sem.at[peer], br_sem.at[peer], (px, peer)
        ).wait()

    def margin_copy(side):
        size = OVMAX * own
        src = base if side == 0 else block * own
        dst = base + block * own if side == 0 else 0
        return remote(
            rh.at[pl.ds(src, size)], rh.at[pl.ds(dst, size)], hs_sem.at[side], hr_sem.at[1 - side], to[side]
        )

    def control_copy(side):
        src = HALO if side == 0 else block
        dst = HALO + block if side == 0 else 0
        return remote(
            ce.at[pl.ds(src, HALO)], ce.at[pl.ds(dst, HALO)], cs_sem.at[side], cr_sem.at[1 - side], to[side]
        )

    def exchange(make, arrive):
        for side in (0, 1):
            when_do(has[side], lambda side=side: make(side).start())
        for side in (0, 1):

            @pl.when(has[side])
            def _(side=side):
                make(side).wait_send()
                arrive(side).wait_recv()

    size = OVMAX * own
    exchange(
        margin_copy,
        lambda side: remote(
            rh.at[pl.ds(base, size)],
            rh.at[pl.ds(0 if side == 0 else base + block * own, size)],
            hs_sem.at[side],
            hr_sem.at[side],
            to[side],
        ),
    )
    kind = jnp.where(px == 0, 0, jnp.where(px == nx - 1, 2, 1))
    index = (kind * (OVMAX + 1) + margin[0, 0]) * (OVMAX + 1) + margin[0, 1]
    mats = tab[index]
    width = block + 2 * OVMAX
    right = jnp.concatenate([rh[pl.ds(m, width, stride=own), :] for m in range(own)], axis=1)
    first = jnp.dot(mats[:block, :width], right, precision=HIGH, preferred_element_type=jnp.float32)
    ce[HALO : HALO + block] = first
    exchange(
        control_copy,
        lambda side: remote(
            ce.at[pl.ds(HALO, HALO)],
            ce.at[pl.ds(0 if side == 0 else HALO + block, HALO)],
            cs_sem.at[side],
            cr_sem.at[side],
            to[side],
        ),
    )
    second = jnp.dot(mats[block:], ce[...], precision=HIGH, preferred_element_type=jnp.float32)
    final = 2.0 * first - second
    for m in range(own):
        ctrl_out[pl.ds(m, block, stride=own), :] = final[:, m * zc : (m + 1) * zc]


def per_device(field, diffusivity, velocity, margin):
    cx, cy, nz = field.shape
    nx, ny = lax.axis_size("px"), lax.axis_size("py")
    chunks = 4
    block, own, zc = cx // 2, cy // 2, nz // 2
    mine = block // ny
    zmat = jnp.asarray(z_matrix(nz))
    ymat = jnp.asarray(y_matrix(cy * ny, ny))
    tab = jnp.asarray(schwarz_table(cx * nx, nx))
    f32, bf16 = jnp.float32, jnp.bfloat16
    V, D = pltpu.VMEM, pltpu.SemaphoreType.DMA
    slab = (cx, cy, nz)
    scratch = [
        V((2, cx + 2, cy, nz), f32),
        V(slab, bf16),
        V((3,) + slab, bf16),
        V((cx + 2, cy, nz), f32),
        V(slab, f32),
        V(slab, f32),
        V((cx + 2, cy, nz), f32),
        V(slab, f32),
        V(slab, f32),
        V(slab, f32),
        V((2, STEPS + 2, cx, nz), f32),
        V((2, STEPS + 2, cx, nz), f32),
        V((2, cx, nz), f32),
        V((2, cy, nz), bf16),
        V((2, cy, nz), bf16),
        V((2, 2, cy, nz), f32),
        V((2, 2, cy, nz), f32),
        V((block, cy, nz), f32),
        V((mine, cy + 24, zc), f32),
        V((ny, mine, QROWS, zc), f32),
        V((ny, mine, QROWS, zc), f32),
        V((ny, mine * own, zc), f32),
        V(((block + 2 * OVMAX) * own, zc), f32),
        V((block + 2 * HALO, own * zc), f32),
        V(zmat.shape, f32),
        V(ymat.shape, f32),
        V(tab.shape, f32),
        D((3,)),
        D((3,)),
        D((STEPS, 2)),
        D((STEPS, 2)),
        D((2, 2)),
        D((2, 2)),
        D((STEPS, chunks, 2)),
        D((STEPS, chunks, 2)),
        D((2,)),
        D((2,)),
        D((ny,)),
        D((ny,)),
        D((ny,)),
        D((ny,)),
        D((2,)),
        D((2,)),
        D((2,)),
        D((2,)),
    ]
    hbm = pl.BlockSpec(memory_space=pl.ANY)
    vmem = pl.BlockSpec(memory_space=pltpu.VMEM)
    adv, ctrl = pl.pallas_call(
        functools.partial(kernel, nx, ny, cx, cy, nz, chunks),
        out_shape=(
            jax.ShapeDtypeStruct(slab, f32),
            jax.ShapeDtypeStruct((block * own, zc), f32),
        ),
        in_specs=[pl.BlockSpec(memory_space=pltpu.SMEM)] + [hbm] * 6,
        out_specs=(vmem, vmem),
        scratch_shapes=scratch,
        compiler_params=pltpu.CompilerParams(
            collective_id=0, has_side_effects=True, vmem_limit_bytes=60 * 2**20
        ),
    )(margin, field, diffusivity, velocity, zmat, ymat, tab)
    return adv, ctrl.reshape(block, own, zc)


def solution(mesh):
    placed = (P("px", "py", None), P("px", "py", None), P(None, "px", "py", None), P("px", None))
    return jax.shard_map(
        per_device,
        mesh=mesh,
        in_specs=placed,
        out_specs=(P("px", "py", None), P("px", "py", None)),
        check_vma=False,
    )
```

profile of v0, /device:TPU:1, one launch (start us, length us, event | category | flops | bytes accessed | tf_op | source)
XLA Modules:
  0.0 86.7 jit_solution(4935389048121775957)
XLA Ops:
  0.6 82.1 %shard_map.86 = (f32[64,32,256]{2,1,0:T(8,128)}, f32[512,128]{1,0:T(8,128)}) custom-call(s32[1,2]{1,0:T(1,128)} %margin.1, f32[64,32,256]{2,1,0:T(8,128)} %field.1, bf16[64,32,256]{2,1,0:T(8,128)(2,1)} %kappa.1, bf16[3,64,32,256]{3,2,1,0:T(8,128)(2,1)} %velo.1, f32[256,128]{1,0:T(8,128)} %constant.6.clone.zmat_h, f32[128,192]{1,0:T(8,128)} %constant.7.clone.ymat_h, ...), custom_call_target="tpu_custom_call" | custom-call | tf_op jit(solution)/shard_map/pallas_call | solution.py:553
  82.8 0.0 copy-start
  82.8 3.2 %copy.11 = f32[64,32,256]{2,1,0:T(8,128)} copy(f32[64,32,256]{2,1,0:T(8,128)} %get-tuple-element.8) | data formatting | bytes 4194304
  86.0 0.0 copy-done
  86.0 0.7 copy.12
Async XLA Ops:
  82.8 3.2 %copy-start = (f32[512,128]{1,0:T(8,128)S(1)}, f32[512,128]{1,0:T(8,128)}, u32[]{:S(2)}) copy-start(f32[512,128]{1,0:T(8,128)} %get-tuple-element.5) | copy-start | bytes 786436
where the time goes:
time: 86.9 us; the launch traced here: 86.7 us
  Pallas kernels  82.1 us (94%)
  local copies, waits for them, and re-layouts  3.91 us (4%)
    pallas_call x1, Pallas kernels, per_device(): pl.pallas_call(functools.partial(kernel, nx, ny, cx, cy, nz, chunks), out...  82.1 us
    unnamed x4, local copies, waits for them, and re-layouts  3.91 us

commit v1 on v0

--- a/solution.py
+++ b/solution.py
@@ -12,7 +12,7 @@
 OVMAX = 4
 HALO = 8
 QROWS = 24
-HIGH = lax.Precision.HIGHEST
+UNROLL = 4
 MESH = pl.DeviceIdType.MESH
 
 
@@ -79,11 +79,26 @@
     return out.reshape(-1, 2 * block, block + 2 * HALO).astype(np.float32)
 
 
+def split(a):
+    top = a.astype(jnp.bfloat16)
+    return top, (a - top.astype(jnp.float32)).astype(jnp.bfloat16)
+
+
+def product(a, b):
+    dot = functools.partial(jnp.dot, preferred_element_type=jnp.float32)
+    return dot(a[0], b[0]) + (dot(a[0], b[1]) + dot(a[1], b[0]))
+
+
+def halves(a):
+    top = a.astype(jnp.bfloat16)
+    return jnp.asarray(np.stack([top, (a - top.astype(np.float32)).astype(jnp.bfloat16)]))
+
+
 def kernel(
     nx, ny, cx, cy, nz, chunks,
     margin, field, kappa, velo, zmat_h, ymat_h, tab_h,
     adv, ctrl_out,
-    U, kb, vb, kk, ky, kz, hx, hy, hz, hzp, ys, yr, gy, kxr, hxr,
+    U, kb, vb, kk, ky, kz, hx, hy, hz, ys, yr, gy, kxr, hxr,
     xps, xpr, xc, zf, a2s, a2r, bs, rh, ce, zmat, ymat, tab,
     in_sem, cst_sem, xs_sem, xr_sem, ki_s, ki_r, ys_sem, yr_sem, ps_sem, pr_sem,
     as_sem, ar_sem, bs_sem, br_sem, hs_sem, hr_sem, cs_sem, cr_sem,
@@ -120,6 +135,7 @@
     ce[0:HALO] = jnp.zeros((HALO, own * zc), jnp.float32)
     ce[HALO + block :] = jnp.zeros((HALO, own * zc), jnp.float32)
     zf[...] = jnp.zeros(zf.shape, jnp.float32)
+    a2r[...] = jnp.zeros(a2r.shape, jnp.float32)
 
     barrier = pltpu.get_barrier_semaphore()
 
@@ -215,9 +231,7 @@
         c.wait()
 
     lane = lax.broadcasted_iota(jnp.int32, (cy, nz), 1)
-    row = lax.broadcasted_iota(jnp.int32, (cy, nz), 0)
-    last_lane, first_lane = lane == nz - 1, lane == 0
-    last_row, first_row = row == cy - 1, row == 0
+    last_lane = lane == nz - 1
 
     def prepare(x):
         k = kb[x].astype(jnp.float32) * 0.05
@@ -229,7 +243,6 @@
         hy[x] = h
         g = vb[2, x].astype(jnp.float32) * 0.025
         hz[x] = g
-        hzp[x] = jnp.where(last_lane, 0.0, pltpu.roll(g, nz - 1, 1))
         u = U[0, x + 1]
         at = pl.ds(x, 1)
         for side, pick in ((0, slice(0, 1)), (1, slice(cy - 1, cy))):
@@ -257,9 +270,21 @@
         kk[at] = kxr[side].astype(jnp.float32) * 0.05
         hx[at] = hxr[side].astype(jnp.float32) * 0.025
 
-    def x_flux(s, x):
-        u, up = U[s, x], U[s, x + 1]
-        return (kk[x] + kk[x + 1]) * (up - u) - (hx[x] * (u * u) + hx[x + 1] * (up * up))
+    tiles = [(slice(8 * i, 8 * i + 8), slice(128 * j, 128 * j + 128)) for i in range(cy // 8) for j in range(nz // 128)]
+    high, wide = cy // 8, nz // 128
+    trow = lax.broadcasted_iota(jnp.int32, (8, 128), 0)
+    tlane = lax.broadcasted_iota(jnp.int32, (8, 128), 1)
+    row_end, row_start = trow == 7, trow == 0
+    lane_end, lane_start = tlane == 127, tlane == 0
+
+    def x_start(s, x):
+        flux, force = [], []
+        for a, b in tiles:
+            u, up = U[s, x, a, b], U[s, x + 1, a, b]
+            fp = hx[x + 1, a, b] * (up * up)
+            flux.append((kk[x, a, b] + kk[x + 1, a, b]) * (up - u) - (hx[x, a, b] * (u * u) + fp))
+            force.append(fp)
+        return tuple(flux), tuple(force)
 
     def partial(side):
         for q in range(2):
@@ -292,31 +317,75 @@
                     ys[side, 1, part] * (a * a) + yr[side, 1, part] * (b * b)
                 )
 
-            def line(i, flux, t=t, s=s, c=c, last=last):
-                x = c * rows + i
-                u, k = U[s, x + 1], kk[x + 1]
-                up = U[s, x + 2]
-                sq = u * u
-                gx = (k + kk[x + 2]) * (up - u) - (hx[x + 1] * sq + hx[x + 2] * (up * up))
-                fy = hy[x] * sq
-                g = ky[x] * (pltpu.roll(u, cy - 1, 0) - u) - (fy + pltpu.roll(fy, cy - 1, 0))
+            def line(x, carry, s=s):
+                flux, force = carry
                 at = pl.ds(x, 1)
-                g = jnp.where(last_row, gy[1, at], g)
-                gym = jnp.where(first_row, gy[0, at], pltpu.roll(g, 1, 0))
-                uz = jnp.where(last_lane, 0.0, pltpu.roll(u, nz - 1, 1))
-                fz = hz[x] * sq
-                gz = kz[x] * (uz - u) - (fz + hzp[x] * (uz * uz))
-                gzm = jnp.where(first_lane, k * u - fz, pltpu.roll(gz, 1, 1))
-                new = u + ((gx - flux) + (g - gym) + (gz - gzm))
-                if last:
-                    adv[x] = new
-                else:
-                    U[1 - s, x + 1] = new
-                    ys[0, t + 3, at] = new[0:1]
-                    ys[1, t + 3, at] = new[cy - 1 : cy]
-                return gx
-
-            lax.fori_loop(0, rows, line, x_flux(s, c * rows))
+                n = len(tiles)
+                low_face, top_face = gy[0, at], gy[1, at]
+                u = [U[s, x + 1, a, b] for a, b in tiles]
+                sq = [v * v for v in u]
+                gx, fx, new = [], [], []
+                for m, (a, b) in enumerate(tiles):
+                    up = U[s, x + 2, a, b]
+                    fp = hx[x + 2, a, b] * (up * up)
+                    g = (kk[x + 1, a, b] + kk[x + 2, a, b]) * (up - u[m]) - (force[m] + fp)
+                    gx.append(g)
+                    fx.append(fp)
+                    new.append(u[m] + (g - flux[m]))
+                ru = [pltpu.roll(v, 7, 0) for v in u]
+                fy = [hy[x, a, b] * sq[m] for m, (a, b) in enumerate(tiles)]
+                rf = [pltpu.roll(v, 7, 0) for v in fy]
+                before = [None] * wide
+                for m, (a, b) in enumerate(tiles):
+                    j = m % wide
+                    if m + wide < n:
+                        up = jnp.where(row_end, ru[m + wide], ru[m])
+                        fp = jnp.where(row_end, rf[m + wide], rf[m])
+                    else:
+                        up, fp = ru[m], rf[m]
+                    g = ky[x, a, b] * (up - u[m]) - (fy[m] + fp)
+                    if m + wide >= n:
+                        g = jnp.where(row_end, top_face[:, b], g)
+                    rg = pltpu.roll(g, 1, 0)
+                    low = low_face[:, b] if m < wide else before[j]
+                    new[m] = new[m] + (g - jnp.where(row_start, low, rg))
+                    before[j] = rg
+                for r in range(high):
+                    fz = [hz[x, a, b] * sq[r * wide + j] for j, (a, b) in enumerate(tiles[r * wide : r * wide + wide])]
+                    ru = [pltpu.roll(u[r * wide + j], 127, 1) for j in range(wide)]
+                    rf = [pltpu.roll(v, 127, 1) for v in fz]
+                    prev = None
+                    for j in range(wide):
+                        m = r * wide + j
+                        a, b = tiles[m]
+                        up = jnp.where(lane_end, ru[j + 1] if j + 1 < wide else 0.0, ru[j])
+                        fp = jnp.where(lane_end, rf[j + 1] if j + 1 < wide else 0.0, rf[j])
+                        g = kz[x, a, b] * (up - u[m]) - (fz[j] + fp)
+                        rg = pltpu.roll(g, 1, 1)
+                        low = kk[x + 1, a, b] * u[m] - fz[j] if j == 0 else prev
+                        new[m] = new[m] + (g - jnp.where(lane_start, low, rg))
+                        prev = rg
+                return new, (tuple(gx), tuple(fx))
+
+            def lines(i, carry, t=t, s=s, c=c, last=last):
+                fresh = []
+                for r in range(UNROLL):
+                    x = c * rows + UNROLL * i + r
+                    new, carry = line(x, carry)
+                    fresh.append((x, new))
+                for x, new in fresh:
+                    at = pl.ds(x, 1)
+                    for m, (a, b) in enumerate(tiles):
+                        if last:
+                            adv[x, a, b] = new[m]
+                        else:
+                            U[1 - s, x + 1, a, b] = new[m]
+                    if not last:
+                        ys[0, t + 3, at] = jnp.concatenate([v[0:1] for v in new[:wide]], axis=1)
+                        ys[1, t + 3, at] = jnp.concatenate([v[7:8] for v in new[-wide:]], axis=1)
+                return carry
+
+            lax.fori_loop(0, rows // UNROLL, lines, x_start(s, c * rows))
             if not last:
                 for side in (0, 1):
                     when_do(hasy[side], lambda t=t, c=c, side=side: y_face(t + 1, c, side).start())
@@ -377,7 +446,7 @@
     def group(peer):
         first = peer * mine
         lines = xc[pl.ds(first, mine)].reshape(mine * cy, nz)
-        fitted = jnp.dot(lines, zmat[...], precision=HIGH, preferred_element_type=jnp.float32)
+        fitted = product(split(lines), (zmat[0], zmat[1]))
         zf[:, 8 : 8 + cy, :] = fitted.reshape(mine, cy, zc)
         for a in range(mine):
             total = None
@@ -386,8 +455,10 @@
                 total = term if total is None else total + term
             a2s[peer, a] = total
 
+    used = pl.ds(0, own + 4)
+
     def a2a(peer):
-        return remote(a2s.at[peer], a2r.at[py], as_sem.at[peer], ar_sem.at[py], (px, peer))
+        return remote(a2s.at[peer, :, used], a2r.at[py, :, used], as_sem.at[peer], ar_sem.at[py], (px, peer))
 
     @pl.loop(1, ny)
     def _(d):
@@ -401,10 +472,10 @@
     @pl.loop(1, ny)
     def _(d):
         peer = lax.rem(py + d, ny)
-        remote(a2s.at[peer], a2r.at[peer], as_sem.at[peer], ar_sem.at[peer], (px, peer)).wait()
+        remote(a2s.at[peer, :, used], a2r.at[peer, :, used], as_sem.at[peer], ar_sem.at[peer], (px, peer)).wait()
 
     gathered = jnp.concatenate([a2r[:, a].reshape(ny * QROWS, zc) for a in range(mine)], axis=1)
-    solved = jnp.dot(ymat[...], gathered, precision=HIGH, preferred_element_type=jnp.float32)
+    solved = product((ymat[0], ymat[1]), split(gathered))
     for q in range(ny):
         for a in range(mine):
             bs[q, a * own : (a + 1) * own] = solved[q * own : (q + 1) * own, a * zc : (a + 1) * zc]
@@ -471,7 +542,7 @@
     mats = tab[index]
     width = block + 2 * OVMAX
     right = jnp.concatenate([rh[pl.ds(m, width, stride=own), :] for m in range(own)], axis=1)
-    first = jnp.dot(mats[:block, :width], right, precision=HIGH, preferred_element_type=jnp.float32)
+    first = product(split(mats[:block, :width]), split(right))
     ce[HALO : HALO + block] = first
     exchange(
         control_copy,
@@ -483,7 +554,7 @@
             to[side],
         ),
     )
-    second = jnp.dot(mats[block:], ce[...], precision=HIGH, preferred_element_type=jnp.float32)
+    second = product(split(mats[block:]), split(ce[...]))
     final = 2.0 * first - second
     for m in range(own):
         ctrl_out[pl.ds(m, block, stride=own), :] = final[:, m * zc : (m + 1) * zc]
@@ -495,8 +566,8 @@
     chunks = 4
     block, own, zc = cx // 2, cy // 2, nz // 2
     mine = block // ny
-    zmat = jnp.asarray(z_matrix(nz))
-    ymat = jnp.asarray(y_matrix(cy * ny, ny))
+    zmat = halves(z_matrix(nz))
+    ymat = halves(y_matrix(cy * ny, ny))
     tab = jnp.asarray(schwarz_table(cx * nx, nx))
     f32, bf16 = jnp.float32, jnp.bfloat16
     V, D = pltpu.VMEM, pltpu.SemaphoreType.DMA
@@ -509,7 +580,6 @@
         V(slab, f32),
         V(slab, f32),
         V((cx + 2, cy, nz), f32),
-        V(slab, f32),
         V(slab, f32),
         V(slab, f32),
         V((2, STEPS + 2, cx, nz), f32),
@@ -526,8 +596,8 @@
         V((ny, mine * own, zc), f32),
         V(((block + 2 * OVMAX) * own, zc), f32),
         V((block + 2 * HALO, own * zc), f32),
-        V(zmat.shape, f32),
-        V(ymat.shape, f32),
+        V(zmat.shape, bf16),
+        V(ymat.shape, bf16),
         V(tab.shape, f32),
         D((3,)),
         D((3,)),
@@ -548,7 +618,7 @@
         D((2,)),
         D((2,)),
     ]
-    hbm = pl.BlockSpec(memory_space=pl.ANY)
+    hbm = pl.BlockSpec(memory_space=pltpu.HBM)
     vmem = pl.BlockSpec(memory_space=pltpu.VMEM)
     adv, ctrl = pl.pallas_call(
         functools.partial(kernel, nx, ny, cx, cy, nz, chunks),
@@ -560,7 +630,7 @@
         out_specs=(vmem, vmem),
         scratch_shapes=scratch,
         compiler_params=pltpu.CompilerParams(
-            collective_id=0, has_side_effects=True, vmem_limit_bytes=60 * 2**20
+            collective_id=0, has_side_effects=True, vmem_limit_bytes=57 * 2**20
         ),
     )(margin, field, diffusivity, velocity, zmat, ymat, tab)
     return adv, ctrl.reshape(block, own, zc)

time: 86.9 us -> 62.1 us (0.71)
  Pallas kernels: 82.1 us -> 57.4 us
    pallas_call x1, Pallas kernels: 82.1 us -> 57.4 us  [per_device(): pl.pallas_call(functools.partial(kernel, nx, ny, cx, cy, nz, chunks), out...]
where the time goes in v1:
time: 62.1 us; the launch traced here: 62 us
  Pallas kernels  57.4 us (92%)
  local copies, waits for them, and re-layouts  3.91 us (6%)
  between operations  0.65 us (1%)
    pallas_call x1, Pallas kernels, per_device(): pl.pallas_call(functools.partial(kernel, nx, ny, cx, cy, nz, chunks), out...  57.4 us
    unnamed x4, local copies, waits for them, and re-layouts  3.91 us

profile of v1, /device:TPU:1, one launch (start us, length us, event | category | flops | bytes accessed | tf_op | source)
XLA Modules:
  0.0 62.0 jit_solution(17020727327791291096)
XLA Ops:
  0.6 57.4 %shard_map.86 = (f32[64,32,256]{2,1,0:T(8,128)}, f32[512,128]{1,0:T(8,128)}) custom-call(s32[1,2]{1,0:T(1,128)} %margin.1, f32[64,32,256]{2,1,0:T(8,128)} %field.1, bf16[64,32,256]{2,1,0:T(8,128)(2,1)} %kappa.1, bf16[3,64,32,256]{3,2,1,0:T(8,128)(2,1)} %velo.1, bf16[2,256,128]{2,1,0:T(8,128)(2,1)} %constant.6.clone.zmat_h, ...), custom_call_target="tpu_custom_call" | custom-call | tf_op jit(solution)/shard_map/pallas_call | solution.py:623
  58.1 0.0 copy-start
  58.1 3.2 %copy.11 = f32[64,32,256]{2,1,0:T(8,128)} copy(f32[64,32,256]{2,1,0:T(8,128)} %get-tuple-element.8) | data formatting | bytes 4194304
  61.3 0.0 copy-done
  61.3 0.7 %copy.12 = f32[32,16,128]{2,1,0:T(8,128)} copy(f32[32,16,128]{2,1,0:T(8,128)S(1)} %bitcast.1) | data formatting | bytes 524288
Async XLA Ops:
  58.1 3.2 %copy-start = (f32[512,128]{1,0:T(8,128)S(1)}, f32[512,128]{1,0:T(8,128)}, u32[]{:S(2)}) copy-start(f32[512,128]{1,0:T(8,128)} %get-tuple-element.5) | copy-start | bytes 786436

commit v2 on v1

--- a/solution.py
+++ b/solution.py
@@ -97,10 +97,10 @@
 def kernel(
     nx, ny, cx, cy, nz, chunks,
     margin, field, kappa, velo, zmat_h, ymat_h, tab_h,
-    adv, ctrl_out,
-    U, kb, vb, kk, ky, kz, hx, hy, hz, ys, yr, gy, kxr, hxr,
+    adv_h, ctrl_out,
+    adv, U, kb, vb, kk, ky, kz, hx, hy, hz, ys, yr, gy, kxr, hxr,
     xps, xpr, xc, zf, a2s, a2r, bs, rh, ce, zmat, ymat, tab,
-    in_sem, cst_sem, xs_sem, xr_sem, ki_s, ki_r, ys_sem, yr_sem, ps_sem, pr_sem,
+    out_sem, in_sem, cst_sem, xs_sem, xr_sem, ki_s, ki_r, ys_sem, yr_sem, ps_sem, pr_sem,
     as_sem, ar_sem, bs_sem, br_sem, hs_sem, hr_sem, cs_sem, cr_sem,
 ):
     px, py = lax.axis_index("px"), lax.axis_index("py")
@@ -252,9 +252,10 @@
 
     for c in range(chunks):
 
-        @pl.loop(0, rows)
+        @pl.loop(0, rows // UNROLL)
         def _(i, c=c):
-            prepare(c * rows + i)
+            for r in range(UNROLL):
+                prepare(c * rows + UNROLL * i + r)
 
         for side in (0, 1):
             when_do(hasy[side], lambda c=c, side=side: y_face(0, c, side).start())
@@ -412,6 +413,9 @@
                 for c in range(chunks):
                     y_face(t, c, side).wait_send()
 
+    leaving = pltpu.make_async_copy(adv, adv_h, out_sem.at[0])
+    leaving.start()
+
     def x_row(k, low, high):
         total = None
         for j in range(8):
@@ -425,9 +429,11 @@
     for k in (block - 2, block - 1):
         xc[k] = x_row(k, 0, cx - 2 * k + 3)
 
-    @pl.loop(2, block - 2)
-    def _(k):
-        xc[k] = x_row(k, 0, 8)
+    @pl.loop(0, (block - 4) // UNROLL)
+    def _(i):
+        for r in range(UNROLL):
+            k = 2 + UNROLL * i + r
+            xc[k] = x_row(k, 0, 8)
 
     for side in (0, 1):
 
@@ -556,6 +562,7 @@
     )
     second = product(split(mats[block:]), split(ce[...]))
     final = 2.0 * first - second
+    leaving.wait()
     for m in range(own):
         ctrl_out[pl.ds(m, block, stride=own), :] = final[:, m * zc : (m + 1) * zc]
 
@@ -564,6 +571,7 @@
     cx, cy, nz = field.shape
     nx, ny = lax.axis_size("px"), lax.axis_size("py")
     chunks = 4
+    assert cx % (chunks * UNROLL) == 0 and (cx // 2 - 4) % UNROLL == 0
     block, own, zc = cx // 2, cy // 2, nz // 2
     mine = block // ny
     zmat = halves(z_matrix(nz))
@@ -573,6 +581,7 @@
     V, D = pltpu.VMEM, pltpu.SemaphoreType.DMA
     slab = (cx, cy, nz)
     scratch = [
+        V(slab, f32),
         V((2, cx + 2, cy, nz), f32),
         V(slab, bf16),
         V((3,) + slab, bf16),
@@ -599,6 +608,7 @@
         V(zmat.shape, bf16),
         V(ymat.shape, bf16),
         V(tab.shape, f32),
+        D((1,)),
         D((3,)),
         D((3,)),
         D((STEPS, 2)),
@@ -627,7 +637,7 @@
             jax.ShapeDtypeStruct((block * own, zc), f32),
         ),
         in_specs=[pl.BlockSpec(memory_space=pltpu.SMEM)] + [hbm] * 6,
-        out_specs=(vmem, vmem),
+        out_specs=(hbm, vmem),
         scratch_shapes=scratch,
         compiler_params=pltpu.CompilerParams(
             collective_id=0, has_side_effects=True, vmem_limit_bytes=57 * 2**20

time: 62.1 us -> 60.8 us (0.979)
  Pallas kernels: 57.4 us -> 55.8 us
    pallas_call x1, Pallas kernels: 57.4 us -> 55.8 us  [per_device(): pl.pallas_call(functools.partial(kernel, nx, ny, cx, cy, nz, chunks), out...]
where the time goes in v2:
time: 60.8 us; the launch traced here: 60.3 us
  Pallas kernels  55.8 us (92%)
  local copies, waits for them, and re-layouts  3.91 us (6%)
  between operations  0.65 us (1%)
    pallas_call x1, Pallas kernels, per_device(): pl.pallas_call(functools.partial(kernel, nx, ny, cx, cy, nz, chunks), out...  55.8 us
    unnamed x4, local copies, waits for them, and re-layouts  3.91 us

profile of v2, /device:TPU:1, one launch (start us, length us, event | category | flops | bytes accessed | tf_op | source)
XLA Modules:
  0.0 60.3 jit_solution(5715399574595944306)
XLA Ops:
  0.6 55.8 %shard_map.86 = (f32[64,32,256]{2,1,0:T(8,128)}, f32[512,128]{1,0:T(8,128)}) custom-call(s32[1,2]{1,0:T(1,128)} %margin.1, f32[64,32,256]{2,1,0:T(8,128)} %field.1, bf16[64,32,256]{2,1,0:T(8,128)(2,1)} %kappa.1, bf16[3,64,32,256]{3,2,1,0:T(8,128)(2,1)} %velo.1, bf16[2,256,128]{2,1,0:T(8,128)(2,1)} %constant.6.clone.zmat_h, ...), custom_call_target="tpu_custom_call" | custom-call | tf_op jit(solution)/shard_map/pallas_call | solution.py:633
  56.4 0.0 copy-start
  56.4 3.2 %copy.11 = f32[64,32,256]{2,1,0:T(8,128)} copy(f32[64,32,256]{2,1,0:T(8,128)} %get-tuple-element.8) | data formatting | bytes 4194304
  59.6 0.0 copy-done
  59.6 0.7 %copy.12 = f32[32,16,128]{2,1,0:T(8,128)} copy(f32[32,16,128]{2,1,0:T(8,128)S(1)} %bitcast.1) | data formatting | bytes 524288
Async XLA Ops:
  56.4 3.2 %copy-start = (f32[512,128]{1,0:T(8,128)S(1)}, f32[512,128]{1,0:T(8,128)}, u32[]{:S(2)}) copy-start(f32[512,128]{1,0:T(8,128)} %get-tuple-element.5) | copy-start | bytes 786436
